TPU v7x, 128 devices: a whole 4x4x4 slice. The times are simulated.
128 devices in a mesh: expert: 8 (over y, z_lo), fsdp: 16 (over x, z_hi, core).
Axes of the slice: x: 4, y: 4, z: 4 (z_hi: 2, z_lo: 2; z = z_hi * 2 + z_lo), core: 2. Of those that a mesh axis runs over, the one named last changes fastest.
Arguments:
- tokens: bfloat16 [18432, 2048], P(('expert', 'fsdp')), may hold values from -6 to 6
- expert_ids: int32 [18432, 6], P(('expert', 'fsdp')), may hold values from 0 to 15, as said below
- combine: float32 [18432, 6], P(('expert', 'fsdp')), may hold values from 0.05 to 1
- gate_weight: bfloat16 [16, 1408, 2048], P('expert', 'fsdp'), may hold values from -0.125 to 0.125
- up_weight: bfloat16 [16, 1408, 2048], P('expert', 'fsdp'), may hold values from -0.125 to 0.125
- down_weight: bfloat16 [16, 1408, 2048], P('expert', 'fsdp'), may hold values from -0.15625 to 0.15625
Outputs:
- mixed: bfloat16 [18432, 2048], P(('expert', 'fsdp'))
Inputs may be any that keep to these rules, and one draw needn't show every extreme that they name: `expert_ids`: each row names 6 different experts. Within the 144 rows of each device no expert is named more than 72 times, and one and the same expert is named exactly 72 times by the rows of every device.
All inputs are finite; a program needn't handle non-finite values.
Results may differ from a plain program's by a relative error of at most 0.0058.
Values may be sent and summed in bfloat16 or wider, within the bound.
A program may use at most 128 MiB of HBM per device.

v0:
```python
import jax
import jax.numpy as jnp
from jax import lax
from jax.sharding import PartitionSpec as P

CAP = 72


def add_piece(expert_rows, pieces):
    gate_piece, up_piece, down_piece = pieces
    gate_pre = jnp.einsum(
        "grd,gfd->grf", expert_rows, gate_piece, preferred_element_type=jnp.float32
    )
    up_pre = jnp.einsum("grd,gfd->grf", expert_rows, up_piece, preferred_element_type=jnp.float32)
    hidden = (jax.nn.silu(gate_pre) * up_pre).astype(jnp.bfloat16)
    return jnp.einsum("grf,gfd->grd", hidden, down_piece, preferred_element_type=jnp.float32)


def per_device(tokens, expert_ids, combine, gate_weight, up_weight, down_weight):
    groups = lax.axis_size("expert")
    per_group = gate_weight.shape[0]
    tok_rows, top_k = expert_ids.shape
    model_width = tokens.shape[1]
    flat_ids = expert_ids.reshape(-1)
    onehot = (flat_ids[:, None] == jnp.arange(per_group * groups, dtype=jnp.int32)[None, :]).astype(
        jnp.int32
    )
    earlier = jnp.cumsum(onehot, axis=0) - onehot
    rank_within = jnp.sum(earlier * onehot, axis=1)
    owner_group = flat_ids // per_group
    within = flat_ids % per_group
    slot_index = (within * groups + owner_group) * CAP + rank_within
    source = jnp.arange(tok_rows * top_k, dtype=jnp.int32) // top_k
    outgoing = (
        jnp.zeros((per_group * groups * CAP, model_width), jnp.bfloat16)
        .at[slot_index]
        .set(tokens[source])
    )
    outgoing = outgoing.reshape(per_group, groups, CAP, model_width)
    arrived = lax.all_to_all(outgoing, "expert", split_axis=1, concat_axis=1, tiled=True)
    expert_rows = arrived.reshape(per_group, groups * CAP, model_width)
    summed = add_piece(
        expert_rows,
        (
            lax.all_gather(gate_weight, "fsdp", axis=1, tiled=True),
            lax.all_gather(up_weight, "fsdp", axis=1, tiled=True),
            lax.all_gather(down_weight, "fsdp", axis=1, tiled=True),
        ),
    )
    produced = summed.astype(jnp.bfloat16)
    produced = produced.reshape(per_group, groups, CAP, model_width)
    returned = lax.all_to_all(produced, "expert", split_axis=1, concat_axis=1, tiled=True)
    back_rows = returned.reshape(per_group * groups * CAP, model_width)[slot_index]
    weighted = (
        back_rows.astype(jnp.float32).reshape(tok_rows, top_k, model_width) * combine[:, :, None]
    )
    return jnp.sum(weighted, axis=1).astype(jnp.bfloat16)


def solution(mesh):
    return jax.shard_map(
        per_device,
        mesh=mesh,
        in_specs=(
            P(("expert", "fsdp"), None),
            P(("expert", "fsdp"), None),
            P(("expert", "fsdp"), None),
            P("expert", "fsdp", None),
            P("expert", "fsdp", None),
            P("expert", "fsdp", None),
        ),
        out_specs=P(("expert", "fsdp"), None),
        check_vma=False,
    )
```

profile of v0, /device:TPU:1, one launch (start us, length us, event | category | flops | bytes accessed | tf_op | source)
XLA Modules:
  0.0 457.1 jit_solution(14942654767058175792)
XLA Ops:
  6.5 0.7 all-gather.4.cloned.1.call-update
  7.3 0.7 all-gather.6.cloned.1.call-update
  8.1 0.7 all-gather.8.cloned.1.call-update
  8.7 0.8 copy.21
  9.5 0.1 eq.24
  9.7 0.1 reshape.195
  9.9 2.0 reduce-window.6
  11.9 0.3 slice_reduce_fusion
  12.4 23.2 %scatter_custom_fusion = bf16[1152,2048]{1,0:T(8,128)(2,1)} fusion(s32[864]{0:T(1024)S(1)} %fusion.5, bf16[144,2048]{1,0:T(8,128)(2,1)S(1)} %copy-done, s32[1024]{0:T(1024)S(1)} %pad_clamp_fusion.1, bf16[]{:T(256)} %constant.42.clone.1), kind=kCustom, calls=%fused_computation.6 | custom fusion | bytes 4718594 | tf_op jit(solution)/shard_map/scatter | solution.py:37
  35.6 2.8 copy.25
  38.4 66.5 %all_to_all.10 = bf16[2,8,72,2048]{3,2,0,1:T(8,128)(2,1)S(1)} all-to-all(bf16[2,8,72,2048]{3,2,0,1:T(8,128)(2,1)S(1)} %copy.25), channel_id=1, replica_groups=mesh['expert'=8,'fsdp'=16] {'expert'}, dimensions={1} | all-to-all | bytes 9437184 | tf_op jit(solution)/shard_map/all_to_all | solution.py:40
  104.9 2.5 copy.26
  107.4 38.9 %all-gather.4.cloned.1.call-done = bf16[2,1408,2048]{2,1,0:T(8,128)(2,1)} async-done(((bf16[2,88,2048]{2,1,0:T(8,128)(2,1)}), bf16[2,1408,2048]{2,1,0:T(8,128)(2,1)}) %all-gather.4.cloned.1.call-update) | async-done | bytes 11534352 | tf_op jit(solution)/shard_map/all_gather | solution.py:45
  146.3 14.4 %fusion.9 = f32[2,576,1408]{2,1,0:T(8,128)} fusion(bf16[2,576,2048]{2,1,0:T(8,128)(2,1)} %bitcast.33, bf16[2,1408,2048]{2,1,0:T(8,128)(2,1)} %all-gather.4.cloned.1.call-done), kind=kOutput, calls=%fused_computation.36 | convolution fusion | flops 6643777536 | bytes 22740992 | tf_op jit(solution)/shard_map/grd,gfd->grf/dot_general | solution.py:11
  160.7 71.9 %all-gather.6.cloned.1.call-done = bf16[2,1408,2048]{2,1,0:T(8,128)(2,1)} async-done(((bf16[2,88,2048]{2,1,0:T(8,128)(2,1)}), bf16[2,1408,2048]{2,1,0:T(8,128)(2,1)}) %all-gather.6.cloned.1.call-update) | async-done | bytes 11534352 | tf_op jit(solution)/shard_map/all_gather | solution.py:46
  232.6 86.3 %all-gather.8.cloned.1.call-done = bf16[2,1408,2048]{2,1,0:T(8,128)(2,1)} async-done(((bf16[2,88,2048]{2,1,0:T(8,128)(2,1)}), bf16[2,1408,2048]{2,1,0:T(8,128)(2,1)}) %all-gather.8.cloned.1.call-update) | async-done | bytes 11534352 | tf_op jit(solution)/shard_map/all_gather | solution.py:47
  318.8 22.8 %convolution_convert_fusion = bf16[2,576,2048]{2,1,0:T(8,128)(2,1)} fusion(bf16[2,1408,2048]{2,1,0:T(8,128)(2,1)} %all-gather.8.cloned.1.call-done, f32[2,576,1408]{2,1,0:T(8,128)} %fusion.9, bf16[2,576,2048]{2,1,0:T(8,128)(2,1)} %bitcast.34, bf16[2,1408,2048]{2,1,0:T(8,128)(2,1)} %all-gather.6.cloned.1.call-done), kind=kOutput, calls=%fused_computation.5 | convolution fusion | flops 13299646464 | bytes 38993920 | tf_op jit(solution)/shard_map/grf,gfd->grd/dot_general | solution.py:16
  341.6 5.2 %copy.27 = bf16[2,8,72,2048]{3,2,0,1:T(8,128)(2,1)} copy(bf16[2,8,72,2048]{3,2,1,0:T(8,128)(2,1)} %bitcast.35) | data formatting | bytes 9437184 | tf_op jit(solution)/shard_map/reshape | solution.py:51
  346.9 4.9 %all-to-all-start.1 = ((bf16[2,8,72,2048]{3,2,0,1:T(8,128)(2,1)}), bf16[2,8,72,2048]{3,2,0,1:T(8,128)(2,1)}, u32[]{:S(2)}, u32[]{:S(2)}) async-start(bf16[2,8,72,2048]{3,2,0,1:T(8,128)(2,1)} %copy.27), calls=%async_computation.1 | async-start | bytes 9437184 | tf_op jit(solution)/shard_map/all_to_all | solution.py:52
  351.9 66.3 %all-to-all-done.1 = bf16[2,8,72,2048]{3,2,0,1:T(8,128)(2,1)} async-done(((bf16[2,8,72,2048]{3,2,0,1:T(8,128)(2,1)}), bf16[2,8,72,2048]{3,2,0,1:T(8,128)(2,1)}, u32[]{:S(2)}, u32[]{:S(2)}) %all-to-all-start.1) | async-done | bytes 4718624 | tf_op jit(solution)/shard_map/all_to_all | solution.py:52
  418.2 5.2 %copy.28 = bf16[2,8,72,2048]{3,2,1,0:T(8,128)(2,1)} copy(bf16[2,8,72,2048]{3,2,0,1:T(8,128)(2,1)} %all-to-all-done.1) | data formatting | bytes 9437184 | tf_op jit(solution)/shard_map/all_to_all | solution.py:52
  423.5 11.7 %gather_fusion = bf16[864,2048]{1,0:T(8,128)(2,1)} fusion(bf16[1152,2048]{1,0:T(8,128)(2,1)} %bitcast.31, s32[1024]{0:T(1024)S(1)} %pad_clamp_fusion), kind=kCustom, calls=%fused_computation.1 | custom fusion | bytes 7081344 | tf_op jit(solution)/shard_map/gather | solution.py:53
  435.2 7.2 %reshape.203 = f32[144,6,2048]{2,1,0:T(8,128)} reshape(bf16[864,2048]{1,0:T(8,128)(2,1)} %gather_fusion) | data formatting | bytes 10616832 | tf_op jit(solution)/shard_map/convert_element_type | solution.py:55
  442.4 8.2 %multiply_reduce_fusion = bf16[144,2048]{1,0:T(8,128)(2,1)} fusion(f32[144,6,2048]{2,1,0:T(8,128)} %reshape.203, f32[144,6]{1,0:T(8,128)S(1)} %copy.29), kind=kLoop, calls=%fused_computation.3 | loop fusion | flops 3244032 | bytes 7671168 | tf_op jit(solution)/shard_map/reduce_sum | solution.py:57
  (19 shorter events, 0.4 us)
Async XLA Ops:
  6.5 5.9 %copy-start = (bf16[144,2048]{1,0:T(8,128)(2,1)S(1)}, bf16[144,2048]{1,0:T(8,128)(2,1)}, u32[]{:S(2)}) copy-start(bf16[144,2048]{1,0:T(8,128)(2,1)} %param.6) | copy-start | bytes 1769476
  6.5 139.8 %all-gather.4.cloned.1.call-start = ((), (), s32[]{:S(2)}) async-start(), calls=%async_computation.2 | async-start | bytes 12255232 | tf_op jit(solution)/shard_map/all_gather | solution.py:45
  7.3 225.3 %all-gather.6.cloned.1.call-start = ((), (), s32[]{:S(2)}) async-start(), calls=%async_computation.3 | async-start | bytes 12255232 | tf_op jit(solution)/shard_map/all_gather | solution.py:46
  8.0 310.8 %all-gather.8.cloned.1.call-start = ((), (), s32[]{:S(2)}) async-start(), calls=%async_computation.4 | async-start | bytes 12255232 | tf_op jit(solution)/shard_map/all_gather | solution.py:47
  346.9 5.0 %copy-start.2 = (f32[144,6]{0,1:T(8,128)S(1)}, f32[144,6]{0,1:T(8,128)}, u32[]{:S(2)}) copy-start(f32[144,6]{0,1:T(8,128)} %param.8) | copy-start | bytes 10372
  346.9 71.4 %all-to-all-start.1 = ((bf16[2,8,72,2048]{3,2,0,1:T(8,128)(2,1)}), bf16[2,8,72,2048]{3,2,0,1:T(8,128)(2,1)}, u32[]{:S(2)}, u32[]{:S(2)}) async-start(bf16[2,8,72,2048]{3,2,0,1:T(8,128)(2,1)} %copy.27), calls=%async_computation.1 | async-start | bytes 9437184 | tf_op jit(solution)/shard_map/all_to_all | solution.py:52
  435.2 15.4 %copy-start.1 = (bf16[144,2048]{1,0:T(8,128)(2,1)S(1)}, bf16[144,2048]{1,0:T(8,128)(2,1)}, u32[]{:S(2)}) copy-start(bf16[144,2048]{1,0:T(8,128)(2,1)} %param.6) | copy-start | bytes 1769476
Sparse Core Ops, SparseCore 0:
  9.8 136.4 all-gather.3
  148.8 83.7 all-gather.5
  235.1 83.7 all-gather.7
where the time goes:
time: 458 us; the launch traced here: 457 us
  waiting for transfers between devices  265 us (58%)
  blocking collectives  66.5 us (15%)
  local copies, waits for them, and re-layouts  59.3 us (13%)
  matrix products  37.2 us (8%)
  between operations  13.2 us (3%)
  other arithmetic  10.4 us (2%)
  starting transfers between devices  5.02 us (1%)
    all_gather x1, waiting for transfers between devices, per_device(): lax.all_gather(down_weight, 'fsdp', axis=1, tiled=True)  86.3 us
    all_gather x1, waiting for transfers between devices, per_device(): lax.all_gather(up_weight, 'fsdp', axis=1, tiled=True)  71.9 us
    all_to_all x1, blocking collectives, per_device(): lax.all_to_all(outgoing, 'expert', split_axis=1, concat_axis=1, tiled=True)  66.5 us
    all_to_all x1, waiting for transfers between devices, per_device(): lax.all_to_all(produced, 'expert', split_axis=1, concat_axis=1, tiled=True)  66.3 us
    all_gather x1, waiting for transfers between devices, per_device(): lax.all_gather(gate_weight, 'fsdp', axis=1, tiled=True)  38.9 us
    scatter x1, local copies, waits for them, and re-layouts, per_device(): outgoing = jnp.zeros((per_group * groups * CAP, model_width), jnp.bfloat1...  23.2 us
    dot_general x1, matrix products, add_piece(): jnp.einsum('grf,gfd->grd', hidden, down_piece, preferred_element_type=jnp...  22.8 us
    dot_general x1, matrix products, add_piece(): jnp.einsum('grd,gfd->grf', expert_rows, gate_piece, preferred_element_typ...  14.4 us
  transfers between devices with their start and end apart: 4, of which 4 were waited for; matrix products, arithmetic and copies ran while one was open for 10% of the time, Pallas kernels for 0%

commit v1 on v0

--- a/solution.py
+++ b/solution.py
@@ -49,7 +49,12 @@
     )
     produced = summed.astype(jnp.bfloat16)
     produced = produced.reshape(per_group, groups, CAP, model_width)
-    returned = lax.all_to_all(produced, "expert", split_axis=1, concat_axis=1, tiled=True)
+    returned = jnp.concatenate(
+        lax.all_to_all(
+            jnp.stack(jnp.split(produced, lax.axis_size("expert"), axis=1)), "expert", 0, 0
+        ),
+        axis=1,
+    )
     back_rows = returned.reshape(per_group * groups * CAP, model_width)[slot_index]
     weighted = (
         back_rows.astype(jnp.float32).reshape(tok_rows, top_k, model_width) * combine[:, :, None]

time: 458 us -> 464 us (1.013)
  local copies, waits for them, and re-layouts: 59.3 us -> 65.6 us
    unnamed x8 -> x17, local copies, waits for them, and re-layouts: 0.91 us -> 11.5 us
    all_to_all x1 -> x0, local copies, waits for them, and re-layouts: 5.23 us -> none  [per_device(): lax.all_to_all(produced, 'expert', split_axis=1, concat_axis=1, tiled=True)]
where the time goes in v1:
time: 464 us; the launch traced here: 463 us
  waiting for transfers between devices  265 us (57%)
  blocking collectives  66.5 us (14%)
  local copies, waits for them, and re-layouts  65.6 us (14%)
  matrix products  37.2 us (8%)
  between operations  13.2 us (3%)
  other arithmetic  10.4 us (2%)
  starting transfers between devices  5.02 us (1%)
    all_gather x1, waiting for transfers between devices, per_device(): lax.all_gather(down_weight, 'fsdp', axis=1, tiled=True)  86.3 us
    all_gather x1, waiting for transfers between devices, per_device(): lax.all_gather(up_weight, 'fsdp', axis=1, tiled=True)  71.9 us
    all_to_all x1, blocking collectives, per_device(): lax.all_to_all(outgoing, 'expert', split_axis=1, concat_axis=1, tiled=True)  66.5 us
    all_to_all x1, waiting for transfers between devices, per_device(): lax.all_to_all(jnp.stack(jnp.split(produced, lax.axis_size('expert'), axi...  66.3 us
    all_gather x1, waiting for transfers between devices, per_device(): lax.all_gather(gate_weight, 'fsdp', axis=1, tiled=True)  38.9 us
    scatter x1, local copies, waits for them, and re-layouts, per_device(): outgoing = jnp.zeros((per_group * groups * CAP, model_width), jnp.bfloat1...  23.2 us
    dot_general x1, matrix products, add_piece(): jnp.einsum('grf,gfd->grd', hidden, down_piece, preferred_element_type=jnp...  22.8 us
    dot_general x1, matrix products, add_piece(): jnp.einsum('grd,gfd->grf', expert_rows, gate_piece, preferred_element_typ...  14.4 us
  transfers between devices with their start and end apart: 4, of which 4 were waited for; matrix products, arithmetic and copies ran while one was open for 10% of the time, Pallas kernels for 0%

profile of v1, /device:TPU:1, one launch (start us, length us, event | category | flops | bytes accessed | tf_op | source)
XLA Modules:
  0.0 463.4 jit_solution(16629838561561609754)
XLA Ops:
  9.9 2.0 reduce-window.6
  12.4 23.2 %scatter_custom_fusion = bf16[1152,2048]{1,0:T(8,128)(2,1)} fusion(s32[864]{0:T(1024)S(1)} %fusion.13, bf16[144,2048]{1,0:T(8,128)(2,1)S(1)} %copy-done, s32[1024]{0:T(1024)S(1)} %get-tuple-element.6, bf16[]{:T(256)} %constant.42.clone.1), kind=kCustom, calls=%fused_computation.6 | custom fusion | bytes 4718594 | tf_op jit(solution)/shard_map/scatter | solution.py:37
  35.6 2.8 copy.47
  38.4 66.5 %all_to_all.10 = bf16[2,8,72,2048]{3,2,0,1:T(8,128)(2,1)S(1)} all-to-all(bf16[2,8,72,2048]{3,2,0,1:T(8,128)(2,1)S(1)} %copy.47), channel_id=1, replica_groups=mesh['expert'=8,'fsdp'=16] {'expert'}, dimensions={1} | all-to-all | bytes 9437184 | tf_op jit(solution)/shard_map/all_to_all | solution.py:40
  104.9 2.5 copy.48
  107.4 38.9 %all-gather.4.cloned.1.call-done = bf16[2,1408,2048]{2,1,0:T(8,128)(2,1)} async-done(((bf16[2,88,2048]{2,1,0:T(8,128)(2,1)}), bf16[2,1408,2048]{2,1,0:T(8,128)(2,1)}) %all-gather.4.cloned.1.call-update) | async-done | bytes 11534352 | tf_op jit(solution)/shard_map/all_gather | solution.py:45
  146.3 14.4 %fusion.17 = f32[2,576,1408]{2,1,0:T(8,128)} fusion(bf16[2,576,2048]{2,1,0:T(8,128)(2,1)} %bitcast.80, bf16[2,1408,2048]{2,1,0:T(8,128)(2,1)} %all-gather.4.cloned.1.call-done), kind=kOutput, calls=%fused_computation.52 | convolution fusion | flops 6643777536 | bytes 22740992 | tf_op jit(solution)/shard_map/grd,gfd->grf/dot_general | solution.py:11
  160.7 71.9 %all-gather.6.cloned.1.call-done = bf16[2,1408,2048]{2,1,0:T(8,128)(2,1)} async-done(((bf16[2,88,2048]{2,1,0:T(8,128)(2,1)}), bf16[2,1408,2048]{2,1,0:T(8,128)(2,1)}) %all-gather.6.cloned.1.call-update) | async-done | bytes 11534352 | tf_op jit(solution)/shard_map/all_gather | solution.py:46
  232.6 86.3 %all-gather.8.cloned.1.call-done = bf16[2,1408,2048]{2,1,0:T(8,128)(2,1)} async-done(((bf16[2,88,2048]{2,1,0:T(8,128)(2,1)}), bf16[2,1408,2048]{2,1,0:T(8,128)(2,1)}) %all-gather.8.cloned.1.call-update) | async-done | bytes 11534352 | tf_op jit(solution)/shard_map/all_gather | solution.py:47
  318.8 22.8 %convolution_convert_fusion = bf16[2,576,2048]{2,1,0:T(8,128)(2,1)} fusion(bf16[2,1408,2048]{2,1,0:T(8,128)(2,1)} %all-gather.8.cloned.1.call-done, f32[2,576,1408]{2,1,0:T(8,128)} %fusion.17, bf16[2,576,2048]{2,1,0:T(8,128)(2,1)} %bitcast.81, bf16[2,1408,2048]{2,1,0:T(8,128)(2,1)} %all-gather.6.cloned.1.call-done), kind=kOutput, calls=%fused_computation.5 | convolution fusion | flops 13299646464 | bytes 38993920 | tf_op jit(solution)/shard_map/grf,gfd->grd/dot_general | solution.py:16
  341.6 2.1 fusion.10
  343.7 1.9 fusion.9
  345.7 1.9 fusion.8
  347.6 1.9 fusion.7
  349.6 0.9 fusion.6
  350.4 0.9 fusion.5
  351.3 0.9 fusion.4
  352.2 1.0 fusion.3
  353.2 4.9 %all-to-all-start.1 = ((bf16[8,2,1,72,2048]{4,3,1,2,0:T(8,128)(2,1)}), bf16[8,2,1,72,2048]{4,3,1,2,0:T(8,128)(2,1)}, u32[]{:S(2)}, u32[]{:S(2)}) async-start(bf16[8,2,1,72,2048]{4,3,1,2,0:T(8,128)(2,1)} %fusion.3), calls=%async_computation.1 | async-start | bytes 9437184 | tf_op jit(solution)/shard_map/all_to_all | solution.py:53
  358.3 66.3 %all-to-all-done.1 = bf16[8,2,1,72,2048]{4,3,1,2,0:T(8,128)(2,1)} async-done(((bf16[8,2,1,72,2048]{4,3,1,2,0:T(8,128)(2,1)}), bf16[8,2,1,72,2048]{4,3,1,2,0:T(8,128)(2,1)}, u32[]{:S(2)}, u32[]{:S(2)}) %all-to-all-start.1) | async-done | bytes 4718624 | tf_op jit(solution)/shard_map/all_to_all | solution.py:53
  424.6 5.2 %copy.56 = bf16[2,8,1,72,2048]{4,3,1,0,2:T(8,128)(2,1)} copy(bf16[2,8,1,72,2048]{4,3,0,2,1:T(8,128)(2,1)} %bitcast.12) | data formatting | bytes 9437184 | tf_op jit(solution)/shard_map/reshape | solution.py:52
  429.8 11.7 %gather_fusion = bf16[864,2048]{1,0:T(8,128)(2,1)} fusion(bf16[1152,2048]{1,0:T(8,128)(2,1)} %bitcast.78, s32[1024]{0:T(1024)S(1)} %get-tuple-element.5), kind=kCustom, calls=%fused_computation.1 | custom fusion | bytes 7081344 | tf_op jit(solution)/shard_map/gather | solution.py:58
  441.5 7.2 %reshape.203 = f32[144,6,2048]{2,1,0:T(8,128)} reshape(bf16[864,2048]{1,0:T(8,128)(2,1)} %gather_fusion) | data formatting | bytes 10616832 | tf_op jit(solution)/shard_map/convert_element_type | solution.py:60
  448.7 8.2 %multiply_reduce_fusion = bf16[144,2048]{1,0:T(8,128)(2,1)} fusion(f32[144,6,2048]{2,1,0:T(8,128)} %reshape.203, f32[144,6]{1,0:T(8,128)S(1)} %copy.57), kind=kLoop, calls=%fused_computation.3 | loop fusion | flops 3244032 | bytes 7671168 | tf_op jit(solution)/shard_map/reduce_sum | solution.py:62
  (27 shorter events, 3.9 us)
Async XLA Ops:
  6.5 5.9 %copy-start = (bf16[144,2048]{1,0:T(8,128)(2,1)S(1)}, bf16[144,2048]{1,0:T(8,128)(2,1)}, u32[]{:S(2)}) copy-start(bf16[144,2048]{1,0:T(8,128)(2,1)} %param.6) | copy-start | bytes 1769476
  6.5 139.8 %all-gather.4.cloned.1.call-start = ((), (), s32[]{:S(2)}) async-start(), calls=%async_computation.2 | async-start | bytes 12255232 | tf_op jit(solution)/shard_map/all_gather | solution.py:45
  7.3 225.3 %all-gather.6.cloned.1.call-start = ((), (), s32[]{:S(2)}) async-start(), calls=%async_computation.3 | async-start | bytes 12255232 | tf_op jit(solution)/shard_map/all_gather | solution.py:46
  8.0 310.8 %all-gather.8.cloned.1.call-start = ((), (), s32[]{:S(2)}) async-start(), calls=%async_computation.4 | async-start | bytes 12255232 | tf_op jit(solution)/shard_map/all_gather | solution.py:47
  341.6 7.9 %copy-start.2 = (bf16[2,576,2048]{2,1,0:T(8,128)(2,1)S(1)}, bf16[2,576,2048]{2,1,0:T(8,128)(2,1)}, u32[]{:S(2)}) copy-start(bf16[2,576,2048]{2,1,0:T(8,128)(2,1)} %convolution_convert_fusion) | copy-start | bytes 14155780
  353.2 5.0 %copy-start.3 = (f32[144,6]{0,1:T(8,128)S(1)}, f32[144,6]{0,1:T(8,128)}, u32[]{:S(2)}) copy-start(f32[144,6]{0,1:T(8,128)} %param.8) | copy-start | bytes 10372
  353.2 71.4 %all-to-all-start.1 = ((bf16[8,2,1,72,2048]{4,3,1,2,0:T(8,128)(2,1)}), bf16[8,2,1,72,2048]{4,3,1,2,0:T(8,128)(2,1)}, u32[]{:S(2)}, u32[]{:S(2)}) async-start(bf16[8,2,1,72,2048]{4,3,1,2,0:T(8,128)(2,1)} %fusion.3), calls=%async_computation.1 | async-start | bytes 9437184 | tf_op jit(solution)/shard_map/all_to_all | solution.py:53
  441.5 15.4 %copy-start.1 = (bf16[144,2048]{1,0:T(8,128)(2,1)S(1)}, bf16[144,2048]{1,0:T(8,128)(2,1)}, u32[]{:S(2)}) copy-start(bf16[144,2048]{1,0:T(8,128)(2,1)} %param.6) | copy-start | bytes 1769476
Sparse Core Ops, SparseCore 0:
  9.8 136.4 all-gather.3
  148.8 83.7 all-gather.5
  235.1 83.7 all-gather.7
